TPU v7x, 256 devices: a whole 4x4x8 slice. The times are simulated.
256 devices in a mesh: pair: 2 (over core), virt: 4 (over x), integ: 32 (over y, z).
Axes of the slice: x: 4, y: 4, z: 8, core: 2. Of those that a mesh axis runs over, the one named last changes fastest.
Arguments:
- amplitudes: bfloat16 [2, 32, 256, 256], P('pair', 'integ', 'virt'), may hold values from -4 to 4
- vv_factors: bfloat16 [512, 256, 256], P('integ'), may hold values from -0.25 to 0.25
- ov_factors: bfloat16 [512, 32, 256], P(None, 'integ'), may hold values from -0.75 to 0.75
- occ_energy_i: float32 [2], P('pair'), may hold values from -2 to -0.5
- occ_energy_j: float32 [32], P('integ'), may hold values from -2 to -0.5
- virt_energy: float32 [256], replicated, may hold values from 0.2 to 3
- vv_mask: int32 [2, 2], replicated, may hold values 0 or 1
- pair_domain: int32 [2, 32, 2], P('pair', 'integ'), may hold values 0 or 1
Outputs:
- update: bfloat16 [2, 32, 256, 256], P('pair', 'integ', 'virt')
All inputs are finite; a program needn't handle non-finite values. No bound on the sum of `pair_domain` on one device may be relied on, other than what follows from the above.
Results may differ from a plain program's by a relative error of at most 0.014.
Values may be sent and summed in bfloat16 or wider, within the bound.
No kernel may reach another device: no remote copies, remote signals or barrier semaphores. Data moves between devices by JAX's collectives and lax.ppermute only.
A program may use at most 64 MiB of HBM per device.

v0:
```python
import jax
import jax.numpy as jnp
from jax import lax
from jax.sharding import PartitionSpec as P

TILE_SIZE = 128


def split_halves(values):
    upper = values.astype(jnp.bfloat16)
    lower = (values - upper.astype(jnp.float32)).astype(jnp.bfloat16)
    return (upper, lower)


def body(
    amplitudes,
    vv_factors,
    ov_factors,
    occ_energy_i,
    occ_energy_j,
    virt_energy,
    vv_mask,
    pair_domain,
):
    share = amplitudes.shape[2]
    virt_index = lax.axis_index("virt")
    row_start = virt_index * share
    domain = jnp.repeat(pair_domain[0, 0], TILE_SIZE).astype(jnp.float32)
    domain_rows = lax.dynamic_slice_in_dim(domain, row_start, share, 0)
    masked = (amplitudes[0, 0].astype(jnp.float32) * domain_rows[:, None] * domain[None, :]).astype(
        jnp.bfloat16
    )
    grid = jnp.repeat(jnp.repeat(vv_mask, TILE_SIZE, axis=0), TILE_SIZE, axis=1).astype(
        jnp.bfloat16
    )
    factors = vv_factors * grid[None]
    factor_rows = lax.dynamic_slice_in_dim(factors, row_start, share, 1)
    masked_block = masked[None, None]
    full_rows = lax.all_gather(masked_block, "virt", axis=2, tiled=True)
    own_pair = full_rows[0, 0]
    all_pairs = lax.all_gather(full_rows, "integ", axis=1, tiled=True)[0]
    columns = lax.dynamic_slice_in_dim(own_pair, row_start, share, 1)
    mixed = (2.0 * masked.astype(jnp.float32) - columns.T.astype(jnp.float32)).astype(jnp.bfloat16)
    own_ov = ov_factors[:, 0, :]
    partial_zeta = jnp.einsum("ac,qc->aq", mixed, own_ov, preferred_element_type=jnp.float32)
    pieces = []
    for first in range(0, lax.axis_size("integ") * 1, 8):
        width = min(8, lax.axis_size("integ") * 1 - first)
        block = lax.dynamic_slice_in_dim(all_pairs, first, width, 0)
        weighted = jnp.einsum(
            "qac,jcd->jqad", factor_rows, block, preferred_element_type=jnp.float32
        ).astype(jnp.bfloat16)
        pieces.append(
            jnp.einsum("jqad,qbd->jab", weighted, factors, preferred_element_type=jnp.float32)
        )
    term = jnp.concatenate(pieces, axis=0)
    ladder = lax.psum_scatter(
        term.astype(jnp.bfloat16), "integ", scatter_dimension=0, tiled=True
    ).astype(jnp.float32)[0]
    zeta = lax.psum(partial_zeta, "integ")
    upper, lower = split_halves(zeta)
    cycle = jnp.dot(upper, own_ov, preferred_element_type=jnp.float32)
    cycle = cycle + jnp.dot(lower, own_ov, preferred_element_type=jnp.float32)
    total = ladder + cycle
    energy_rows = lax.dynamic_slice_in_dim(virt_energy, row_start, share, 0)
    denom = energy_rows[:, None] + virt_energy[None, :] - occ_energy_i[0] - occ_energy_j[0]
    update = (total * domain_rows[:, None] * domain[None, :] / denom).astype(jnp.bfloat16)
    return update[None, None]


def solution(mesh):
    placed = (
        P("pair", "integ", "virt", None),
        P("integ", None, None),
        P(None, "integ", None),
        P("pair"),
        P("integ"),
        P(),
        P(),
        P("pair", "integ", None),
    )
    return jax.shard_map(
        body,
        mesh=mesh,
        in_specs=placed,
        out_specs=P("pair", "integ", "virt", None),
        check_vma=False,
    )
```

profile of v0, /device:TPU:2, one launch (start us, length us, event | category | flops | bytes accessed | tf_op | source)
XLA Modules:
  0.0 472.5 jit_solution(15324939264644739411)
XLA Ops:
  6.5 0.0 copy-start
  6.5 0.0 all-gather.2.cloned.1.call-start
  6.5 0.7 convert_bitcast_fusion.2
  7.2 0.1 broadcast_bitcast_fusion
  7.3 0.1 dynamic_slice.32
  7.4 0.8 fusion.92
  8.2 12.8 %all_gather.6 = bf16[1,1,256,256]{3,2,1,0:T(8,128)(2,1)} all-gather(bf16[1,1,64,256]{3,2,1,0:T(8,128)(2,1)S(1)} %fusion.92), channel_id=1, replica_groups=mesh['pair'=2,'virt'=4,'integ'=32] {'virt'}, dimensions={2}, use_global_device_ids=true | all-gather | bytes 163840 | tf_op jit(solution)/shard_map/all_gather | solution.py:39
  21.0 0.0 all-gather.2.cloned.1.call-update
  21.1 0.0 all-reduce.2.cloned.1.call-start
  21.1 0.9 constant_dynamic-slice_fusion
  22.1 0.1 copy.22
  22.2 0.0 copy-done
  22.2 1.6 fusion.89
  23.8 0.0 all-reduce.2.cloned.1.call-update
  23.8 0.0 reduce-scatter.2.cloned.1.call-start
  23.9 0.7 convert_element_type.102
  24.6 0.3 broadcast_in_dim.10
  24.9 1.8 broadcast_multiply_fusion
  26.7 78.9 %all-gather.2.cloned.1.call-done = bf16[1,32,256,256]{3,2,0,1:T(8,128)(2,1)} async-done(((bf16[1,1,256,256]{3,2,0,1:T(8,128)(2,1)}), bf16[1,32,256,256]{3,2,0,1:T(8,128)(2,1)}) %all-gather.2.cloned.1.call-update) | async-done | bytes 4194320 | tf_op jit(solution)/shard_map/all_gather | solution.py:41
  105.6 5.4 %fusion.44 = bf16[8,64,256]{2,1,0:T(8,128)(2,1)S(1)} fusion(bf16[16,256,256]{2,1,0:T(8,128)(2,1)S(1)} %broadcast_multiply_fusion, bf16[1,32,256,256]{3,2,0,1:T(8,128)(2,1)} %all-gather.2.cloned.1.call-done, s32[]{:T(128)S(6)} %select_n.2), kind=kOutput, calls=%fused_computation.24 | convolution fusion | flops 2149711872 | bytes 3932164 | tf_op jit(solution)/shard_map/jqad,qbd->jab/dot_general | solution.py:54
  111.1 5.4 %fusion.49 = bf16[8,64,256]{2,1,0:T(8,128)(2,1)S(1)} fusion(bf16[16,256,256]{2,1,0:T(8,128)(2,1)S(1)} %broadcast_multiply_fusion, bf16[1,32,256,256]{3,2,0,1:T(8,128)(2,1)} %all-gather.2.cloned.1.call-done, s32[]{:T(128)S(6)} %select_n.2), kind=kOutput, calls=%fused_computation.25 | convolution fusion | flops 2149711872 | bytes 3932164 | tf_op jit(solution)/shard_map/jqad,qbd->jab/dot_general | solution.py:54
  116.5 5.5 %fusion.54 = bf16[8,64,256]{2,1,0:T(8,128)(2,1)S(1)} fusion(bf16[16,256,256]{2,1,0:T(8,128)(2,1)S(1)} %broadcast_multiply_fusion, bf16[1,32,256,256]{3,2,0,1:T(8,128)(2,1)} %all-gather.2.cloned.1.call-done, s32[]{:T(128)S(6)} %select_n.2), kind=kOutput, calls=%fused_computation.26 | convolution fusion | flops 2149711872 | bytes 3932164 | tf_op jit(solution)/shard_map/jqad,qbd->jab/dot_general | solution.py:54
  122.0 0.0 copy-start.1
  122.0 5.5 %fusion.59 = bf16[8,64,256]{2,1,0:T(8,128)(2,1)S(1)} fusion(bf16[16,256,256]{2,1,0:T(8,128)(2,1)S(1)} %broadcast_multiply_fusion, bf16[1,32,256,256]{3,2,0,1:T(8,128)(2,1)} %all-gather.2.cloned.1.call-done, s32[]{:T(128)S(6)} %select_n.2), kind=kOutput, calls=%fused_computation.27 | convolution fusion | flops 2149711872 | bytes 3932164 | tf_op jit(solution)/shard_map/jqad,qbd->jab/dot_general | solution.py:54
  127.5 1.1 pad_maximum_fusion
  128.6 0.0 reduce-scatter.2.cloned.1.call-update
  128.6 0.0 copy-done.1
  128.6 0.1 dynamic_slice.43
  130.0 117.1 %all-reduce.2.cloned.1.call-done = f32[64,512]{1,0:T(8,128)} async-done(((f32[64,512]{1,0:T(8,128)}), f32[64,512]{1,0:T(8,128)}) %all-reduce.2.cloned.1.call-update) | async-done | bytes 131088 | tf_op jit(solution)/shard_map/psum | solution.py:60
  247.1 1.1 fusion.87
  248.2 216.0 %reduce-scatter.2.cloned.1.call-done = bf16[1,64,256]{2,1,0:T(8,128)(2,1)} async-done(((bf16[32,64,256]{2,1,0:T(8,128)(2,1)}), bf16[1,64,256]{2,1,0:T(8,128)(2,1)}) %reduce-scatter.2.cloned.1.call-update) | async-done | bytes 32784 | tf_op jit(solution)/shard_map/reduce_scatter | solution.py:57
  464.2 1.8 fusion.69
  (2 shorter events, 0.0 us)
Async XLA Ops:
  6.5 15.6 %copy-start = (bf16[512,1,256]{2,0,1:T(8,128)(2,1)S(1)}, bf16[512,1,256]{2,0,1:T(8,128)(2,1)}, u32[]{:S(2)}) copy-start(bf16[512,1,256]{2,0,1:T(8,128)(2,1)} %param.10) | copy-start | bytes 786436
  6.5 99.1 %all-gather.2.cloned.1.call-start = ((), (), s32[]{:S(2)}) async-start(), calls=%async_computation.1 | async-start | bytes 4325376 | tf_op jit(solution)/shard_map/all_gather | solution.py:41
  21.1 226.1 %all-reduce.2.cloned.1.call-start = ((), (), s32[]{:S(2)}) async-start(), calls=%async_computation.3 | async-start | bytes 262144 | tf_op jit(solution)/shard_map/psum | solution.py:60
  23.8 440.4 %reduce-scatter.2.cloned.1.call-start = ((), (), s32[]{:S(2)}) async-start(), calls=%async_computation.2 | async-start | bytes 1081344 | tf_op jit(solution)/shard_map/reduce_scatter | solution.py:57
  122.0 6.6 %copy-start.1 = (f32[256]{0:T(256)S(1)}, f32[256]{0:T(256)}, u32[]{:S(2)}) copy-start(f32[256]{0:T(256)} %param.13) | copy-start | bytes 3076
Sparse Core Ops, SparseCore 0:
  21.2 84.4 all-gather.1
  109.1 137.9 all-reduce.1
  251.4 212.6 reduce-scatter.1
where the time goes:
time: 473 us; the launch traced here: 472 us
  waiting for transfers between devices  412 us (87%)
  matrix products  26.3 us (6%)
  between operations  14.5 us (3%)
  blocking collectives  12.8 us (3%)
  other arithmetic  5.11 us (1%)
    reduce_scatter x1, waiting for transfers between devices, body(): lax.psum_scatter(term.astype(jnp.bfloat16), 'integ', scatter_dimension=0,...  216 us
    psum x1, waiting for transfers between devices, body(): zeta = lax.psum(partial_zeta, 'integ')  117 us
    all_gather x1, waiting for transfers between devices, body(): all_pairs = lax.all_gather(full_rows, 'integ', axis=1, tiled=True)[0]  78.9 us
    dot_general x4, matrix products, body(): jnp.einsum('jqad,qbd->jab', weighted, factors, preferred_element_type=jnp...  21.8 us
    all_gather x1, blocking collectives, body(): full_rows = lax.all_gather(masked_block, 'virt', axis=2, tiled=True)  12.8 us
  transfers between devices with their start and end apart: 3, of which 3 were waited for; matrix products, arithmetic and copies ran while one was open for 6% of the time, Pallas kernels for 0%

commit v1 on v0

--- a/solution.py
+++ b/solution.py
@@ -36,7 +36,9 @@
     factors = vv_factors * grid[None]
     factor_rows = lax.dynamic_slice_in_dim(factors, row_start, share, 1)
     masked_block = masked[None, None]
-    full_rows = lax.all_gather(masked_block, "virt", axis=2, tiled=True)
+    full_rows = jnp.concatenate(
+        lax.all_to_all(jnp.stack([masked_block] * lax.axis_size("virt")), "virt", 0, 0), axis=2
+    )
     own_pair = full_rows[0, 0]
     all_pairs = lax.all_gather(full_rows, "integ", axis=1, tiled=True)[0]
     columns = lax.dynamic_slice_in_dim(own_pair, row_start, share, 1)

time: 473 us -> 469 us (level)
    all_gather x1 -> x0, blocking collectives: 12.8 us -> none  [body(): full_rows = lax.all_gather(masked_block, 'virt', axis=2, tiled=True)]
    all_to_all x0 -> x1, blocking collectives: none -> 9.83 us  [body(): lax.all_to_all(jnp.stack([masked_block] * lax.axis_size('virt')), 'virt',...]
where the time goes in v1:
time: 469 us; the launch traced here: 468 us
  waiting for transfers between devices  412 us (88%)
  matrix products  25.5 us (5%)
  between operations  14.5 us (3%)
  blocking collectives  9.83 us (2%)
  other arithmetic  5.1 us (1%)
    reduce_scatter x1, waiting for transfers between devices, body(): lax.psum_scatter(term.astype(jnp.bfloat16), 'integ', scatter_dimension=0,...  216 us
    psum x1, waiting for transfers between devices, body(): zeta = lax.psum(partial_zeta, 'integ')  117 us
    all_gather x1, waiting for transfers between devices, body(): all_pairs = lax.all_gather(full_rows, 'integ', axis=1, tiled=True)[0]  79.3 us
    dot_general x4, matrix products, body(): jnp.einsum('jqad,qbd->jab', weighted, factors, preferred_element_type=jnp...  21.8 us
    all_to_all x1, blocking collectives, body(): lax.all_to_all(jnp.stack([masked_block] * lax.axis_size('virt')), 'virt',...  9.83 us
  transfers between devices with their start and end apart: 3, of which 3 were waited for; matrix products, arithmetic and copies ran while one was open for 6% of the time, Pallas kernels for 0%

profile of v1, /device:TPU:2, one launch (start us, length us, event | category | flops | bytes accessed | tf_op | source)
XLA Modules:
  0.0 468.3 jit_solution(11141489984104511651)
XLA Ops:
  6.5 0.0 copy-start
  6.5 0.0 all-gather.2.cloned.1.call-start
  6.5 0.7 convert_bitcast_fusion.1
  7.2 0.1 broadcast_bitcast_fusion
  7.3 0.1 dynamic_slice.32
  7.4 0.8 fusion.99
  8.2 9.8 %all_to_all.5 = bf16[4,1,1,64,256]{4,3,2,1,0:T(8,128)(2,1)} all-to-all(bf16[4,1,1,64,256]{4,3,2,1,0:T(8,128)(2,1)S(1)} %stack.3), channel_id=1, replica_groups=mesh['pair'=2,'virt'=4,'integ'=32] {'virt'}, dimensions={0} | all-to-all | bytes 262144 | tf_op jit(solution)/shard_map/all_to_all | solution.py:40
  18.1 0.0 all-gather.2.cloned.1.call-update
  18.1 0.0 all-reduce.2.cloned.1.call-start
  18.2 0.7 convert_element_type.104
  18.9 0.3 broadcast_in_dim.10
  19.2 1.8 broadcast_multiply_fusion
  21.0 0.0 copy-done.1
  21.0 0.1 constant_dynamic-slice_fusion
  21.1 0.1 copy.25
  21.2 0.0 copy-done
  21.2 0.9 fusion.89
  22.1 0.0 all-reduce.2.cloned.1.call-update
  22.1 0.0 reduce-scatter.2.cloned.1.call-start
  22.2 79.3 %all-gather.2.cloned.1.call-done = bf16[1,32,256,256]{3,2,0,1:T(8,128)(2,1)} async-done(((bf16[1,1,256,256]{3,2,0,1:T(8,128)(2,1)}), bf16[1,32,256,256]{3,2,0,1:T(8,128)(2,1)}) %all-gather.2.cloned.1.call-update) | async-done | bytes 4194320 | tf_op jit(solution)/shard_map/all_gather | solution.py:43
  101.5 5.4 %fusion.44 = bf16[8,64,256]{2,1,0:T(8,128)(2,1)S(1)} fusion(bf16[16,256,256]{2,1,0:T(8,128)(2,1)S(1)} %broadcast_multiply_fusion, bf16[1,32,256,256]{3,2,1,0:T(8,128)(2,1)} %bitcast.170, s32[]{:T(128)S(6)} %select_n.2), kind=kOutput, calls=%fused_computation.24 | convolution fusion | flops 2149711872 | bytes 3932164 | tf_op jit(solution)/shard_map/jqad,qbd->jab/dot_general | solution.py:56
  106.9 5.5 %fusion.49 = bf16[8,64,256]{2,1,0:T(8,128)(2,1)S(1)} fusion(bf16[16,256,256]{2,1,0:T(8,128)(2,1)S(1)} %broadcast_multiply_fusion, bf16[1,32,256,256]{3,2,1,0:T(8,128)(2,1)} %bitcast.171, s32[]{:T(128)S(6)} %select_n.2), kind=kOutput, calls=%fused_computation.25 | convolution fusion | flops 2149711872 | bytes 3932164 | tf_op jit(solution)/shard_map/jqad,qbd->jab/dot_general | solution.py:56
  112.4 5.5 %fusion.54 = bf16[8,64,256]{2,1,0:T(8,128)(2,1)S(1)} fusion(bf16[16,256,256]{2,1,0:T(8,128)(2,1)S(1)} %broadcast_multiply_fusion, bf16[1,32,256,256]{3,2,1,0:T(8,128)(2,1)} %bitcast.172, s32[]{:T(128)S(6)} %select_n.2), kind=kOutput, calls=%fused_computation.26 | convolution fusion | flops 2149711872 | bytes 3932164 | tf_op jit(solution)/shard_map/jqad,qbd->jab/dot_general | solution.py:56
  117.9 0.0 copy-start.3
  117.9 5.5 %fusion.59 = bf16[8,64,256]{2,1,0:T(8,128)(2,1)S(1)} fusion(bf16[16,256,256]{2,1,0:T(8,128)(2,1)S(1)} %broadcast_multiply_fusion, bf16[1,32,256,256]{3,2,1,0:T(8,128)(2,1)} %bitcast.173, s32[]{:T(128)S(6)} %select_n.2), kind=kOutput, calls=%fused_computation.27 | convolution fusion | flops 2149711872 | bytes 3932164 | tf_op jit(solution)/shard_map/jqad,qbd->jab/dot_general | solution.py:56
  123.3 1.1 pad_maximum_fusion
  124.4 0.0 reduce-scatter.2.cloned.1.call-update
  124.5 0.1 dynamic_slice.43
  125.9 117.1 %all-reduce.2.cloned.1.call-done = f32[64,512]{1,0:T(8,128)} async-done(((f32[64,512]{1,0:T(8,128)}), f32[64,512]{1,0:T(8,128)}) %all-reduce.2.cloned.1.call-update) | async-done | bytes 131088 | tf_op jit(solution)/shard_map/psum | solution.py:62
  243.0 1.1 fusion.87
  244.0 216.0 %reduce-scatter.2.cloned.1.call-done = bf16[1,64,256]{2,1,0:T(8,128)(2,1)} async-done(((bf16[32,64,256]{2,1,0:T(8,128)(2,1)}), bf16[1,64,256]{2,1,0:T(8,128)(2,1)}) %reduce-scatter.2.cloned.1.call-update) | async-done | bytes 32784 | tf_op jit(solution)/shard_map/reduce_scatter | solution.py:59
  460.0 1.8 fusion.69
  (7 shorter events, 0.0 us)
Async XLA Ops:
  6.5 14.7 %copy-start = (bf16[512,1,256]{2,0,1:T(8,128)(2,1)S(1)}, bf16[512,1,256]{2,0,1:T(8,128)(2,1)}, u32[]{:S(2)}) copy-start(bf16[512,1,256]{2,0,1:T(8,128)(2,1)} %param.10) | copy-start | bytes 786436
  6.5 14.7 %copy-start.2 = (bf16[1,1,64,256]{3,2,1,0:T(8,128)(2,1)S(1)}, bf16[1,1,64,256]{3,2,1,0:T(8,128)(2,1)}, u32[]{:S(2)}) copy-start(bf16[1,1,64,256]{3,2,1,0:T(8,128)(2,1)} %param.8) | copy-start | bytes 98308
  6.5 95.0 %all-gather.2.cloned.1.call-start = ((), (), s32[]{:S(2)}) async-start(), calls=%async_computation.2 | async-start | bytes 4325376 | tf_op jit(solution)/shard_map/all_gather | solution.py:43
  18.1 2.9 copy-start.1
  18.1 224.9 %all-reduce.2.cloned.1.call-start = ((), (), s32[]{:S(2)}) async-start(), calls=%async_computation.4 | async-start | bytes 262144 | tf_op jit(solution)/shard_map/psum | solution.py:62
  22.1 437.9 %reduce-scatter.2.cloned.1.call-start = ((), (), s32[]{:S(2)}) async-start(), calls=%async_computation.3 | async-start | bytes 1081344 | tf_op jit(solution)/shard_map/reduce_scatter | solution.py:59
  117.9 6.6 %copy-start.3 = (f32[256]{0:T(256)S(1)}, f32[256]{0:T(256)}, u32[]{:S(2)}) copy-start(f32[256]{0:T(256)} %param.13) | copy-start | bytes 3076
Sparse Core Ops, SparseCore 0:
  18.2 83.2 all-gather.1
  104.9 137.9 all-reduce.1
  247.3 212.6 reduce-scatter.1

commit v2 on v0

--- a/solution.py
+++ b/solution.py
@@ -57,7 +57,7 @@
     ladder = lax.psum_scatter(
         term.astype(jnp.bfloat16), "integ", scatter_dimension=0, tiled=True
     ).astype(jnp.float32)[0]
-    zeta = lax.psum(partial_zeta, "integ")
+    zeta = jnp.sum(lax.all_gather(partial_zeta, "integ"), axis=0)
     upper, lower = split_halves(zeta)
     cycle = jnp.dot(upper, own_ov, preferred_element_type=jnp.float32)
     cycle = cycle + jnp.dot(lower, own_ov, preferred_element_type=jnp.float32)

time: 473 us -> 411 us (0.87)
  waiting for transfers between devices: 412 us -> 349 us
    psum x1 -> x0, waiting for transfers between devices: 117 us -> none  [body(): zeta = lax.psum(partial_zeta, 'integ')]
    all_gather x0 -> x1, waiting for transfers between devices: none -> 57.3 us  [body(): zeta = jnp.sum(lax.all_gather(partial_zeta, 'integ'), axis=0)]
  transfers between devices with their start and end apart: 3 -> 3, of which waited for: 3 -> 3; matrix products, arithmetic and copies ran while one was open for 6% -> 8% of each run, Pallas kernels for 0% -> 0%
where the time goes in v2:
time: 411 us
  waiting for transfers between devices  349 us (85%)
  matrix products  25.1 us (6%)
  between operations  14.5 us (4%)
  blocking collectives  12.8 us (3%)
  other arithmetic  7.65 us (2%)
    reduce_scatter x1, waiting for transfers between devices, body(): lax.psum_scatter(term.astype(jnp.bfloat16), 'integ', scatter_dimension=0,...  213 us
    all_gather x1, waiting for transfers between devices, body(): all_pairs = lax.all_gather(full_rows, 'integ', axis=1, tiled=True)[0]  78.9 us
    all_gather x1, waiting for transfers between devices, body(): zeta = jnp.sum(lax.all_gather(partial_zeta, 'integ'), axis=0)  57.3 us
    dot_general x4, matrix products, body(): jnp.einsum('jqad,qbd->jab', weighted, factors, preferred_element_type=jnp...  21.8 us
    all_gather x1, blocking collectives, body(): full_rows = lax.all_gather(masked_block, 'virt', axis=2, tiled=True)  12.8 us
  transfers between devices with their start and end apart: 3, of which 3 were waited for; matrix products, arithmetic and copies ran while one was open for 8% of the time, Pallas kernels for 0%

profile of v2, /device:TPU:2, one launch (start us, length us, event | category | flops | bytes accessed | tf_op | source)
XLA Modules:
  0.0 410.9 jit_solution(14737095083376745069)
XLA Ops:
  6.5 0.0 copy-start
  6.5 0.0 all-gather.4.cloned.1.call-start
  6.5 0.7 convert_bitcast_fusion.2
  7.2 0.1 broadcast_bitcast_fusion
  7.3 0.1 dynamic_slice.32
  7.4 0.8 fusion.92
  8.2 12.8 %all_gather.12 = bf16[1,1,256,256]{3,2,1,0:T(8,128)(2,1)} all-gather(bf16[1,1,64,256]{3,2,1,0:T(8,128)(2,1)S(1)} %fusion.92), channel_id=1, replica_groups=mesh['pair'=2,'virt'=4,'integ'=32] {'virt'}, dimensions={2}, use_global_device_ids=true | all-gather | bytes 163840 | tf_op jit(solution)/shard_map/all_gather | solution.py:39
  21.0 0.0 all-gather.4.cloned.1.call-update
  21.1 0.0 all-gather.6.cloned.1.call-start
  21.1 0.9 constant_dynamic-slice_fusion
  22.1 0.1 copy.22
  22.2 1.6 fusion.89
  23.8 0.0 all-gather.6.cloned.1.call-update
  23.8 0.0 reduce-scatter.2.cloned.1.call-start
  23.8 0.7 convert_element_type.102
  24.5 0.3 broadcast_in_dim.10
  24.9 1.8 broadcast_multiply_fusion
  26.7 78.9 %all-gather.4.cloned.1.call-done = bf16[1,32,256,256]{3,2,0,1:T(8,128)(2,1)} async-done(((bf16[1,1,256,256]{3,2,0,1:T(8,128)(2,1)}), bf16[1,32,256,256]{3,2,0,1:T(8,128)(2,1)}) %all-gather.4.cloned.1.call-update) | async-done | bytes 4194320 | tf_op jit(solution)/shard_map/all_gather | solution.py:41
  105.6 5.4 %fusion.44 = bf16[8,64,256]{2,1,0:T(8,128)(2,1)S(1)} fusion(bf16[16,256,256]{2,1,0:T(8,128)(2,1)S(1)} %broadcast_multiply_fusion, bf16[1,32,256,256]{3,2,0,1:T(8,128)(2,1)} %all-gather.4.cloned.1.call-done, s32[]{:T(128)S(6)} %select_n.2), kind=kOutput, calls=%fused_computation.24 | convolution fusion | flops 2149711872 | bytes 3932164 | tf_op jit(solution)/shard_map/jqad,qbd->jab/dot_general | solution.py:54
  111.1 5.4 %fusion.49 = bf16[8,64,256]{2,1,0:T(8,128)(2,1)S(1)} fusion(bf16[16,256,256]{2,1,0:T(8,128)(2,1)S(1)} %broadcast_multiply_fusion, bf16[1,32,256,256]{3,2,0,1:T(8,128)(2,1)} %all-gather.4.cloned.1.call-done, s32[]{:T(128)S(6)} %select_n.2), kind=kOutput, calls=%fused_computation.25 | convolution fusion | flops 2149711872 | bytes 3932164 | tf_op jit(solution)/shard_map/jqad,qbd->jab/dot_general | solution.py:54
  116.5 5.5 %fusion.54 = bf16[8,64,256]{2,1,0:T(8,128)(2,1)S(1)} fusion(bf16[16,256,256]{2,1,0:T(8,128)(2,1)S(1)} %broadcast_multiply_fusion, bf16[1,32,256,256]{3,2,0,1:T(8,128)(2,1)} %all-gather.4.cloned.1.call-done, s32[]{:T(128)S(6)} %select_n.2), kind=kOutput, calls=%fused_computation.26 | convolution fusion | flops 2149711872 | bytes 3932164 | tf_op jit(solution)/shard_map/jqad,qbd->jab/dot_general | solution.py:54
  122.0 0.0 copy-start.1
  122.0 5.4 %fusion.59 = bf16[8,64,256]{2,1,0:T(8,128)(2,1)S(1)} fusion(bf16[16,256,256]{2,1,0:T(8,128)(2,1)S(1)} %broadcast_multiply_fusion, bf16[1,32,256,256]{3,2,0,1:T(8,128)(2,1)} %all-gather.4.cloned.1.call-done, s32[]{:T(128)S(6)} %select_n.2), kind=kOutput, calls=%fused_computation.27 | convolution fusion | flops 2149711872 | bytes 3932164 | tf_op jit(solution)/shard_map/jqad,qbd->jab/dot_general | solution.py:54
  127.5 1.1 pad_maximum_fusion
  128.6 0.0 reduce-scatter.2.cloned.1.call-update
  128.6 0.0 copy-done.1
  128.6 0.1 dynamic_slice.43
  130.0 57.3 %all-gather.6.cloned.1.call-done = f32[2048,512]{1,0:T(8,128)} async-done(((f32[64,512]{1,0:T(8,128)}), f32[2048,512]{1,0:T(8,128)}) %all-gather.6.cloned.1.call-update) | async-done | bytes 4194320 | tf_op jit(solution)/shard_map/all_gather | solution.py:60
  187.3 2.5 reduce_sum.9
  189.8 0.2 fusion.87
  190.0 212.8 %reduce-scatter.2.cloned.1.call-done = bf16[1,64,256]{2,1,0:T(8,128)(2,1)} async-done(((bf16[32,64,256]{2,1,0:T(8,128)(2,1)}), bf16[1,64,256]{2,1,0:T(8,128)(2,1)}) %reduce-scatter.2.cloned.1.call-update) | async-done | bytes 32784 | tf_op jit(solution)/shard_map/reduce_scatter | solution.py:57
  402.8 1.6 fusion.69
  (3 shorter events, 0.0 us)
Async XLA Ops:
  6.5 15.6 %copy-start = (bf16[512,1,256]{2,0,1:T(8,128)(2,1)S(1)}, bf16[512,1,256]{2,0,1:T(8,128)(2,1)}, u32[]{:S(2)}) copy-start(bf16[512,1,256]{2,0,1:T(8,128)(2,1)} %param.10) | copy-start | bytes 786436
  6.5 99.1 %all-gather.4.cloned.1.call-start = ((), (), s32[]{:S(2)}) async-start(), calls=%async_computation.1 | async-start | bytes 4325376 | tf_op jit(solution)/shard_map/all_gather | solution.py:41
  21.1 166.2 %all-gather.6.cloned.1.call-start = ((), (), s32[]{:S(2)}) async-start(), calls=%async_computation.3 | async-start | bytes 4325376 | tf_op jit(solution)/shard_map/all_gather | solution.py:60
  23.8 379.0 %reduce-scatter.2.cloned.1.call-start = ((), (), s32[]{:S(2)}) async-start(), calls=%async_computation.2 | async-start | bytes 1081344 | tf_op jit(solution)/shard_map/reduce_scatter | solution.py:57
  122.0 6.6 %copy-start.1 = (f32[256]{0:T(256)S(1)}, f32[256]{0:T(256)}, u32[]{:S(2)}) copy-start(f32[256]{0:T(256)} %param.13) | copy-start | bytes 3076
Sparse Core Ops, SparseCore 0:
  21.2 84.4 all-gather.3
  108.2 79.0 all-gather.5
  191.1 211.6 reduce-scatter.1
